TPU v7x, 32 devices: a whole 2x2x4 slice. The times are simulated.
32 devices in a mesh: scan: 8 (over z, x), depth: 4 (over y, core).
Axes of the slice: x: 2, y: 2, z: 4, core: 2. Of those that a mesh axis runs over, the one named last changes fastest.
Arguments:
- object_slices: float32 [4, 2, 512, 2048], P('depth', None, 'scan'), may hold values from -1 to 1, as said below
- probe_wave: float32 [2, 128, 128], replicated, may hold values from -4 to 4
- offsets: int32 [128, 2], P('scan'), may hold values from 0 to 1920, as said below
- intensity: float32 [128, 128, 128], P('scan'), may hold values from 0 to 1
Outputs:
- gradient: float32 [4, 2, 512, 2048], P('depth', None, 'scan')
Inputs may be any that keep to these rules, and one draw needn't show every extreme that they name: `offsets`: position k has its row offset between max(0, (k // 16) * 64 - 64) and min(384, (k // 16) * 64 + 2 * 64 - 128), both ends reached on every scan device, and its column offset between 0 and 1920, both reached on every scan device. `object_slices`: each entry has magnitude at most 1.
All inputs are finite; a program needn't handle non-finite values.
Results may differ from a plain program's by a relative error of at most 0.007.
Values may be sent and summed in bfloat16 or wider, within the bound.
A program may use at most 64 MiB of HBM per device.

v0:
```python
import functools
import math

import jax
import jax.numpy as jnp
import numpy as np
from jax import lax
from jax.experimental import pallas as pl
from jax.experimental.pallas import tpu as pltpu
from jax.sharding import PartitionSpec as P

FRESNEL = 0.0024
MESH = pl.DeviceIdType.MESH
HOP_LAG = 3
HALO_TYPE = jnp.float16


def block_tables(extent):
    index = np.arange(extent)
    phases = -2.0 * math.pi / extent * (index[:, None] * index[None, :] % extent)
    real, imag = (np.cos(phases) / math.sqrt(extent), np.sin(phases) / math.sqrt(extent))
    direct = np.block([[real, imag], [-imag, real]]).astype(np.float32)
    conjugated = np.block([[real, -imag], [imag, real]]).astype(np.float32)
    tables = []
    for matrix in (direct, conjugated):
        high = matrix.astype(jnp.bfloat16)
        tables += [high, (matrix - high.astype(np.float32)).astype(jnp.bfloat16)]
    return np.stack(tables)


def kernel_table(extent):
    index = np.arange(extent)
    signed = np.where(index < extent // 2, index, index - extent).astype(np.float64)
    square = signed * signed
    phases = -math.pi * FRESNEL * (square[:, None] + square[None, :])
    return np.stack([np.cos(phases), np.sin(phases)]).astype(np.float32)


def times(first, second):
    return (
        first[0] * second[0] - first[1] * second[1],
        first[0] * second[1] + first[1] * second[0],
    )


def conj_times(first, second):
    return (
        first[0] * second[0] + first[1] * second[1],
        first[0] * second[1] - first[1] * second[0],
    )


def split(value):
    high = value.astype(jnp.bfloat16)
    return high, (value - high.astype(jnp.float32)).astype(jnp.bfloat16)


def dot(first, second):
    return jnp.dot(first, second, preferred_element_type=jnp.float32)


def right_product(field, high, low):
    extent = field[0].shape[1]
    value_high, value_low = split(jnp.concatenate(field, axis=1))
    out = dot(value_high, high) + dot(value_low, high) + dot(value_high, low)
    return out[:, :extent], out[:, extent:]


def left_product(high, low, field):
    extent = field[0].shape[0]
    width = field[0].shape[1]
    value_high, value_low = split(jnp.concatenate(field, axis=0))
    both = dot(high, jnp.concatenate([value_high, value_low], axis=1))
    out = both[:, :width] + both[:, width:] + dot(low, value_high)
    return out[:extent], out[extent:]


def aligned_place(offset, unit, length, taken):
    start = jnp.minimum(offset // unit * unit, length - taken)
    return pl.multiple_of(start, unit), offset - start


def pipeline_kernel(
    sections,
    patches,
    probe_ref,
    intensity_ref,
    tables_ref,
    kernel_ref,
    out_ref,
    psi_in,
    psi_out,
    chi_in,
    chi_out,
    wave,
    own,
    adjoint,
    psi_send,
    psi_recv,
    chi_send,
    chi_recv,
):
    section = lax.axis_index("depth")
    final = sections - 1
    positions, extent = (out_ref.shape[0], out_ref.shape[-1])
    following = lax.rem(section + 1, sections)
    previous = lax.rem(section + sections - 1, sections)

    barrier = pltpu.get_barrier_semaphore()
    for neighbour in (previous, following):
        pl.semaphore_signal(barrier, inc=1, device_id={"depth": neighbour}, device_id_type=MESH)
    pl.semaphore_wait(barrier, 2)

    def psi_copy(index):
        return pltpu.make_async_remote_copy(
            src_ref=psi_out.at[index],
            dst_ref=psi_in.at[index],
            send_sem=psi_send.at[index],
            recv_sem=psi_recv.at[index],
            device_id={"depth": following},
            device_id_type=MESH,
        )

    def chi_copy(index):
        return pltpu.make_async_remote_copy(
            src_ref=chi_out.at[index],
            dst_ref=chi_in.at[index],
            send_sem=chi_send.at[index],
            recv_sem=chi_recv.at[index],
            device_id={"depth": previous},
            device_id_type=MESH,
        )

    def direct():
        return tables_ref[0], tables_ref[1]

    def conjugated():
        return tables_ref[2], tables_ref[3]

    def forward_load(index):
        @pl.when(section == 0)
        def _():
            wave[index] = probe_ref[...]

        @pl.when(section > 0)
        def _():
            psi_copy(index).wait_recv()
            wave[index] = psi_in[index].astype(jnp.float32)

    def forward_compute(index):
        patch = (patches[index, 0], patches[index, 1])
        excited = times(patch, (wave[index, 0], wave[index, 1]))
        far = left_product(*conjugated(), right_product(excited, *direct()))
        misfit = far[0] * far[0] + far[1] * far[1] - intensity_ref[index]
        is_last = section == final
        multiplier = (
            jnp.where(is_last, misfit, kernel_ref[0]),
            jnp.where(is_last, 0.0, kernel_ref[1]),
        )
        result = left_product(
            *direct(), right_product(times(multiplier, far), *conjugated())
        )
        for part in range(2):
            own[lax.rem(index, 2), part] = result[part]
            psi_out[index, part] = result[part].astype(jnp.bfloat16)

    def forward_send(index):
        @pl.when(section < final)
        def _():
            psi_copy(index).start()

    def backward_load(index):
        @pl.when(section == final)
        def _():
            adjoint[...] = own[lax.rem(index, 2)]

        @pl.when(section < final)
        def _():
            chi_copy(index).wait_recv()
            adjoint[...] = chi_in[index].astype(jnp.float32)

    def backward_gradient(index):
        chi = (adjoint[0], adjoint[1])
        term = conj_times((wave[index, 0], wave[index, 1]), chi)
        for part in range(2):
            out_ref[index, part] = term[part]

    def backward_compute(index):
        chi = (adjoint[0], adjoint[1])
        masked = conj_times((patches[index, 0], patches[index, 1]), chi)
        far = left_product(*direct(), right_product(masked, *conjugated()))
        kernel = (kernel_ref[0], kernel_ref[1])
        result = left_product(
            *conjugated(), right_product(conj_times(kernel, far), *direct())
        )
        for part in range(2):
            chi_out[index, part] = result[part].astype(jnp.bfloat16)

    def backward_send(index):
        @pl.when(section > 0)
        def _():
            chi_copy(index).start()

    lag = jnp.minimum(HOP_LAG * (final - section) + 1, positions)

    def forward_only(step, carry):
        forward_load(step)
        forward_compute(step)
        forward_send(step)
        return carry

    def both(step, carry):
        index = step - lag
        forward_load(step)
        backward_load(index)
        forward_compute(step)
        backward_gradient(index)
        backward_compute(index)
        forward_send(step)
        backward_send(index)
        return carry

    def backward_only(step, carry):
        index = step - lag
        backward_load(index)
        backward_gradient(index)

        @pl.when(section > 0)
        def _():
            backward_compute(index)

        backward_send(index)
        return carry

    lax.fori_loop(0, lag, forward_only, 0)
    lax.fori_loop(lag, positions, both, 0)
    lax.fori_loop(positions, positions + lag, backward_only, 0)

    def drain(index, carry):
        @pl.when(section < final)
        def _():
            psi_copy(index).wait_send()

        @pl.when(section > 0)
        def _():
            chi_copy(index).wait_send()

        return carry

    lax.fori_loop(0, positions, drain, 0)


def pipeline(sections, patches, probe, intensity):
    positions, extent = (intensity.shape[0], intensity.shape[-1])
    vmem = pl.BlockSpec(memory_space=pltpu.VMEM)
    waves = (positions, 2, extent, extent)
    semaphores = pltpu.SemaphoreType.DMA((positions,))
    return pl.pallas_call(
        functools.partial(pipeline_kernel, sections),
        out_shape=jax.ShapeDtypeStruct(waves, jnp.float32),
        in_specs=[vmem] * 5,
        out_specs=vmem,
        scratch_shapes=[
            pltpu.VMEM(waves, jnp.bfloat16),
            pltpu.VMEM(waves, jnp.bfloat16),
            pltpu.VMEM(waves, jnp.bfloat16),
            pltpu.VMEM(waves, jnp.bfloat16),
            pltpu.VMEM(waves, jnp.float32),
            pltpu.VMEM((2, 2, extent, extent), jnp.float32),
            pltpu.VMEM((2, extent, extent), jnp.float32),
            semaphores,
            semaphores,
            semaphores,
            semaphores,
        ],
        compiler_params=pltpu.CompilerParams(
            collective_id=0, has_side_effects=True, vmem_limit_bytes=48 * 1024 * 1024
        ),
    )(
        patches,
        probe,
        intensity,
        jnp.asarray(block_tables(extent)),
        jnp.asarray(kernel_table(extent)),
    )


def cut_kernel(rows_ref, cols_ref, layer_ref, out_ref):
    positions, extent = (out_ref.shape[0], out_ref.shape[-1])
    columns = layer_ref.shape[-1]

    def cut_window(index, carry):
        tall, wide = (extent + 8, 2 * extent)
        top, down = aligned_place(rows_ref[index], 8, layer_ref.shape[1], tall)
        start, shift = aligned_place(cols_ref[index], extent, columns, wide)
        for part in range(2):
            block = layer_ref[part, pl.ds(top, tall), pl.ds(start, wide)]
            block = pltpu.roll(block, lax.rem(wide - shift, wide), 1)[:, :extent]
            out_ref[index, part] = pltpu.roll(block, lax.rem(tall - down, tall), 0)[:extent]
        return carry

    lax.fori_loop(0, positions, cut_window, 0)


def cut(row_starts, col_starts, layer, extent):
    smem = pl.BlockSpec(memory_space=pltpu.SMEM)
    vmem = pl.BlockSpec(memory_space=pltpu.VMEM)
    windows = (row_starts.shape[0], 2, extent, extent)
    return pl.pallas_call(
        cut_kernel,
        out_shape=jax.ShapeDtypeStruct(windows, jnp.float32),
        in_specs=[smem, smem, vmem],
        out_specs=vmem,
        compiler_params=pltpu.CompilerParams(vmem_limit_bytes=32 * 1024 * 1024),
    )(row_starts, col_starts, layer)


def scatter_kernel(rows_ref, cols_ref, terms_ref, middle_ref, upper_ref, lower_ref, grid):
    positions, extent = (terms_ref.shape[0], terms_ref.shape[-1])
    columns = grid.shape[-1]
    strip = middle_ref.shape[1]
    grid[...] = jnp.zeros_like(grid)

    def add_window(index, carry):
        tall, wide = (extent + 8, 2 * extent)
        top, down = aligned_place(rows_ref[index], 8, grid.shape[1], tall)
        start, shift = aligned_place(cols_ref[index], extent, columns, wide)
        for part in range(2):
            term = terms_ref[index, part]
            term = jnp.concatenate([term, jnp.zeros((8, extent), term.dtype)], axis=0)
            term = pltpu.roll(term, down, 0)
            term = jnp.concatenate([term, jnp.zeros_like(term)], axis=1)
            place = (part, pl.ds(top, tall), pl.ds(start, wide))
            grid[place] = grid[place] + pltpu.roll(term, shift, 1)
        return carry

    lax.fori_loop(0, positions, add_window, 0)
    upper_ref[...] = grid[:, :strip].astype(upper_ref.dtype)
    middle_ref[...] = grid[:, strip : 2 * strip]
    lower_ref[...] = grid[:, 2 * strip :].astype(lower_ref.dtype)


def scatter(row_starts, col_starts, terms, strip, columns):
    smem = pl.BlockSpec(memory_space=pltpu.SMEM)
    vmem = pl.BlockSpec(memory_space=pltpu.VMEM)
    piece = (2, strip, columns)
    return pl.pallas_call(
        scatter_kernel,
        out_shape=[
            jax.ShapeDtypeStruct(piece, jnp.float32),
            jax.ShapeDtypeStruct(piece, jnp.bfloat16),
            jax.ShapeDtypeStruct(piece, jnp.bfloat16),
        ],
        in_specs=[smem, smem, vmem],
        out_specs=[vmem, vmem, vmem],
        scratch_shapes=[pltpu.VMEM((2, 3 * strip, columns), jnp.float32)],
        compiler_params=pltpu.CompilerParams(vmem_limit_bytes=32 * 1024 * 1024),
    )(row_starts, col_starts, terms)


def shards(scan_peers, sections, object_slices, probe_wave, offsets, intensity):
    layer = object_slices[0]
    strip, columns = layer.shape[1:]
    scan_index = lax.axis_index("scan")
    up = [(i, i + 1) for i in range(scan_peers - 1)]
    down = [(j, i) for i, j in up]
    travelling = layer.astype(HALO_TYPE)
    before = lax.ppermute(travelling, "scan", up)
    after = lax.ppermute(travelling, "scan", down)
    extended = jnp.concatenate(
        [before.astype(jnp.float32), layer, after.astype(jnp.float32)], axis=1
    )
    row_starts = offsets[:, 0] - (scan_index - 1) * strip
    col_starts = offsets[:, 1]
    patches = cut(row_starts, col_starts, extended, probe_wave.shape[-1])
    terms = pipeline(sections, patches, probe_wave, intensity)
    middle, upper, lower = scatter(row_starts, col_starts, terms, strip, columns)
    from_below = lax.ppermute(lower, "scan", up).astype(jnp.float32)
    from_above = lax.ppermute(upper, "scan", down).astype(jnp.float32)
    return (middle + from_below + from_above)[None]


def solution(mesh):
    in_specs = (P("depth", None, "scan", None), P(), P("scan", None), P("scan", None, None))
    out_specs = P("depth", None, "scan", None)
    body = functools.partial(shards, mesh.shape["scan"], mesh.shape["depth"])
    return jax.shard_map(body, mesh=mesh, in_specs=in_specs, out_specs=out_specs, check_vma=False)
```

profile of v0, /device:TPU:0, one launch (start us, length us, event | category | flops | bytes accessed | tf_op | source)
XLA Modules:
  0.0 119.6 jit_solution(15507076329612681143)
XLA Ops:
  0.0 0.0 copy-start.4
  0.0 1.4 %bitcast_convert_fusion = f16[2,64,2048]{2,1,0:T(8,128)(2,1)S(1)} fusion(f32[1,2,64,2048]{3,2,1,0:T(8,128)} %param.6), kind=kLoop, calls=%fused_computation.4 | loop fusion | flops 262144 | bytes 1572864 | tf_op jit(solution)/shard_map/convert_element_type | solution.py:367
  1.4 1.3 %collective-permute-start.1 = (f16[2,64,2048]{2,1,0:T(8,128)(2,1)S(1)}, f16[2,64,2048]{2,1,0:T(8,128)(2,1)S(1)}, u32[]{:S(2)}, u32[]{:S(2)}) collective-permute-start(f16[2,64,2048]{2,1,0:T(8,128)(2,1)S(1)} %bitcast_convert_fusion), channel_id=1, source_target_pairs={{4,0},{8,4},{12,8},{16,12},{20,16},{24,20},{28,24},{5,1},{9,5},{13... | collective-permute-start | bytes 1572872 | tf_op jit(solution)/shard_map/ppermute | solution.py:369
  2.7 5.5 %collective-permute-start = (f16[2,64,2048]{2,1,0:T(8,128)(2,1)S(1)}, f16[2,64,2048]{2,1,0:T(8,128)(2,1)S(1)}, u32[]{:S(2)}, u32[]{:S(2)}) collective-permute-start(f16[2,64,2048]{2,1,0:T(8,128)(2,1)S(1)} %bitcast_convert_fusion), channel_id=1, source_target_pairs={{0,4},{4,8},{8,12},{12,16},{16,20},{20,24},{24,28},{1,5},{5,9},{9,... | collective-permute-start | bytes 1572872 | tf_op jit(solution)/shard_map/ppermute | solution.py:368
  8.2 0.8 slice_bitcast_fusion
  9.0 9.2 %collective-permute-done.1 = f16[2,64,2048]{2,1,0:T(8,128)(2,1)S(1)} collective-permute-done((f16[2,64,2048]{2,1,0:T(8,128)(2,1)S(1)}, f16[2,64,2048]{2,1,0:T(8,128)(2,1)S(1)}, u32[]{:S(2)}, u32[]{:S(2)}) %collective-permute-start.1) | collective-permute-done | bytes 524320 | tf_op jit(solution)/shard_map/ppermute | solution.py:369
  18.1 0.1 convert_element_type.17
  18.2 11.3 %collective-permute-done = f16[2,64,2048]{2,1,0:T(8,128)(2,1)S(1)} collective-permute-done((f16[2,64,2048]{2,1,0:T(8,128)(2,1)S(1)}, f16[2,64,2048]{2,1,0:T(8,128)(2,1)S(1)}, u32[]{:S(2)}, u32[]{:S(2)}) %collective-permute-start) | collective-permute-done | bytes 524320 | tf_op jit(solution)/shard_map/ppermute | solution.py:368
  29.5 0.1 convert_element_type.16
  29.6 0.0 copy-done.4
  29.6 0.2 pad_maximum_fusion.layer_ref
  29.8 0.0 copy-start
  29.8 0.0 copy-start.1
  29.9 0.0 copy-start.2
  29.9 0.0 copy-start.3
  29.9 3.2 %shard_map.64.patches = f32[16,2,128,128]{3,2,1,0:T(8,128)S(1)} custom-call(s32[16]{0:T(128)S(1)} %get-tuple-element.12.rows_ref, s32[16]{0:T(128)S(1)} %get-tuple-element.11.cols_ref, f32[2,192,2048]{2,1,0:T(8,128)S(1)} %pad_maximum_fusion.layer_ref), custom_call_target="tpu_custom_call" | custom-call | tf_op jit(solution)/shard_map/pallas_call | solution.py:309
  33.1 0.0 copy-done
  33.1 0.0 copy-done.1
  33.1 0.0 copy-done.2
  33.1 0.0 copy-done.3
  33.1 55.2 %shard_map.65.terms_ref = f32[16,2,128,128]{3,2,1,0:T(8,128)S(1)} custom-call(f32[16,2,128,128]{3,2,1,0:T(8,128)S(1)} %shard_map.64.patches, f32[2,128,128]{2,1,0:T(8,128)S(1)} %copy-done.2, f32[16,128,128]{2,1,0:T(8,128)S(1)} %copy-done, bf16[4,256,256]{2,1,0:T(8,128)(2,1)S(1)} %copy-done.1, f32[2,128,128]{2,1,0:T(8,128)S(1)} %copy-done.3), custom_call_target="tpu_custom_call" | custom-call | tf_op jit(solution)/shard_map/pallas_call | solution.py:258
  88.3 3.1 %shard_map.66 = (f32[2,64,2048]{2,1,0:T(8,128)S(1)}, bf16[2,64,2048]{2,1,0:T(8,128)(2,1)S(1)}, bf16[2,64,2048]{2,1,0:T(8,128)(2,1)S(1)}) custom-call(s32[16]{0:T(128)S(1)} %get-tuple-element.12.rows_ref, s32[16]{0:T(128)S(1)} %get-tuple-element.11.cols_ref, f32[16,2,128,128]{3,2,1,0:T(8,128)S(1)} %shard_map.65.terms_ref), custom_call_target="tpu_custom_call" | custom-call | tf_op jit(solution)/shard_map/pallas_call | solution.py:347
  91.5 4.4 %collective-permute-start.2 = (bf16[2,64,2048]{2,1,0:T(8,128)(2,1)S(1)}, bf16[2,64,2048]{2,1,0:T(8,128)(2,1)S(1)}, u32[]{:S(2)}, u32[]{:S(2)}) collective-permute-start(bf16[2,64,2048]{2,1,0:T(8,128)(2,1)S(1)} %get-tuple-element.9), channel_id=1, source_target_pairs={{0,4},{4,8},{8,12},{12,16},{16,20},{20,24},{24,28},{1,5},{5,9},{9,... | collective-permute-start | bytes 1572872 | tf_op jit(solution)/shard_map/ppermute | solution.py:378
  95.9 1.3 %collective-permute-start.3 = (bf16[2,64,2048]{2,1,0:T(8,128)(2,1)S(1)}, bf16[2,64,2048]{2,1,0:T(8,128)(2,1)S(1)}, u32[]{:S(2)}, u32[]{:S(2)}) collective-permute-start(bf16[2,64,2048]{2,1,0:T(8,128)(2,1)S(1)} %get-tuple-element.10), channel_id=1, source_target_pairs={{4,0},{8,4},{12,8},{16,12},{20,16},{24,20},{28,24},{5,1},{9,5},{13... | collective-permute-start | bytes 1572872 | tf_op jit(solution)/shard_map/ppermute | solution.py:379
  97.2 21.2 %collective-permute-done.2 = bf16[2,64,2048]{2,1,0:T(8,128)(2,1)S(1)} collective-permute-done((bf16[2,64,2048]{2,1,0:T(8,128)(2,1)S(1)}, bf16[2,64,2048]{2,1,0:T(8,128)(2,1)S(1)}, u32[]{:S(2)}, u32[]{:S(2)}) %collective-permute-start.2) | collective-permute-done | bytes 524320 | tf_op jit(solution)/shard_map/ppermute | solution.py:378
  118.4 0.0 collective-permute-done.3
  118.4 1.2 add_bitcast_fusion
Async XLA Ops:
  0.0 29.6 %copy-start.4 = (f32[1,2,64,2048]{3,2,1,0:T(8,128)S(1)}, f32[1,2,64,2048]{3,2,1,0:T(8,128)}, u32[]{:S(2)}) copy-start(f32[1,2,64,2048]{3,2,1,0:T(8,128)} %param.6) | copy-start | bytes 3145732
  1.4 16.8 %collective-permute-start.1 = (f16[2,64,2048]{2,1,0:T(8,128)(2,1)S(1)}, f16[2,64,2048]{2,1,0:T(8,128)(2,1)S(1)}, u32[]{:S(2)}, u32[]{:S(2)}) collective-permute-start(f16[2,64,2048]{2,1,0:T(8,128)(2,1)S(1)} %bitcast_convert_fusion), channel_id=1, source_target_pairs={{4,0},{8,4},{12,8},{16,12},{20,16},{24,20},{28,24},{5,1},{9,5},{13... | collective-permute-start | bytes 1572872 | tf_op jit(solution)/shard_map/ppermute | solution.py:369
  2.7 26.8 %collective-permute-start = (f16[2,64,2048]{2,1,0:T(8,128)(2,1)S(1)}, f16[2,64,2048]{2,1,0:T(8,128)(2,1)S(1)}, u32[]{:S(2)}, u32[]{:S(2)}) collective-permute-start(f16[2,64,2048]{2,1,0:T(8,128)(2,1)S(1)} %bitcast_convert_fusion), channel_id=1, source_target_pairs={{0,4},{4,8},{8,12},{12,16},{16,20},{20,24},{24,28},{1,5},{5,9},{9,... | collective-permute-start | bytes 1572872 | tf_op jit(solution)/shard_map/ppermute | solution.py:368
  29.8 3.3 %copy-start = (f32[16,128,128]{2,1,0:T(8,128)S(1)}, f32[16,128,128]{2,1,0:T(8,128)}, u32[]{:S(2)}) copy-start(f32[16,128,128]{2,1,0:T(8,128)} %intensity_ref.1) | copy-start | bytes 3145732
  29.8 3.3 %copy-start.1 = (bf16[4,256,256]{2,1,0:T(8,128)(2,1)S(1)}, bf16[4,256,256]{2,1,0:T(8,128)(2,1)}, u32[]{:S(2)}) copy-start(bf16[4,256,256]{2,1,0:T(8,128)(2,1)} %constant.15.clone.tables_ref) | copy-start | bytes 1572868
  29.9 3.3 %copy-start.2 = (f32[2,128,128]{2,1,0:T(8,128)S(1)}, f32[2,128,128]{2,1,0:T(8,128)}, u32[]{:S(2)}) copy-start(f32[2,128,128]{2,1,0:T(8,128)} %probe_ref.1) | copy-start | bytes 393220
  29.9 3.3 %copy-start.3 = (f32[2,128,128]{2,1,0:T(8,128)S(1)}, f32[2,128,128]{2,1,0:T(8,128)}, u32[]{:S(2)}) copy-start(f32[2,128,128]{2,1,0:T(8,128)} %constant.16.clone.kernel_ref) | copy-start | bytes 393220
  91.5 27.0 %collective-permute-start.2 = (bf16[2,64,2048]{2,1,0:T(8,128)(2,1)S(1)}, bf16[2,64,2048]{2,1,0:T(8,128)(2,1)S(1)}, u32[]{:S(2)}, u32[]{:S(2)}) collective-permute-start(bf16[2,64,2048]{2,1,0:T(8,128)(2,1)S(1)} %get-tuple-element.9), channel_id=1, source_target_pairs={{0,4},{4,8},{8,12},{12,16},{16,20},{20,24},{24,28},{1,5},{5,9},{9,... | collective-permute-start | bytes 1572872 | tf_op jit(solution)/shard_map/ppermute | solution.py:378
  95.9 22.6 %collective-permute-start.3 = (bf16[2,64,2048]{2,1,0:T(8,128)(2,1)S(1)}, bf16[2,64,2048]{2,1,0:T(8,128)(2,1)S(1)}, u32[]{:S(2)}, u32[]{:S(2)}) collective-permute-start(bf16[2,64,2048]{2,1,0:T(8,128)(2,1)S(1)} %get-tuple-element.10), channel_id=1, source_target_pairs={{4,0},{8,4},{12,8},{16,12},{20,16},{24,20},{28,24},{5,1},{9,5},{13... | collective-permute-start | bytes 1572872 | tf_op jit(solution)/shard_map/ppermute | solution.py:379
where the time goes:
time: 120 us
  Pallas kernels  61.5 us (51%)
  waiting for transfers between devices  41.7 us (35%)
  starting transfers between devices  12.5 us (10%)
  other arithmetic  3.65 us (3%)
    pallas_call x1, Pallas kernels, pipeline(): pl.pallas_call(functools.partial(pipeline_kernel, sections), out_shape=ja...  55.2 us
    ppermute x1, waiting for transfers between devices, shards(): from_below = lax.ppermute(lower, 'scan', up).astype(jnp.float32)  21.2 us
    ppermute x1, waiting for transfers between devices, shards(): before = lax.ppermute(travelling, 'scan', up)  11.3 us
    ppermute x1, waiting for transfers between devices, shards(): after = lax.ppermute(travelling, 'scan', down)  9.19 us
    ppermute x1, starting transfers between devices, shards(): before = lax.ppermute(travelling, 'scan', up)  5.5 us
    ppermute x1, starting transfers between devices, shards(): from_below = lax.ppermute(lower, 'scan', up).astype(jnp.float32)  4.41 us
    pallas_call x1, Pallas kernels, cut(): pl.pallas_call(cut_kernel, out_shape=jax.ShapeDtypeStruct(windows, jnp.fl...  3.22 us
    pallas_call x1, Pallas kernels, scatter(): pl.pallas_call(scatter_kernel, out_shape=[jax.ShapeDtypeStruct(piece, jnp...  3.12 us
  transfers between devices with their start and end apart: 4, of which 3 were waited for; matrix products, arithmetic and copies ran while one was open for 1% of the time, Pallas kernels for 0%

commit v1 on v0

--- a/solution.py
+++ b/solution.py
@@ -12,7 +12,7 @@
 FRESNEL = 0.0024
 MESH = pl.DeviceIdType.MESH
 HOP_LAG = 3
-HALO_TYPE = jnp.float16
+HALO_TYPE = jnp.bfloat16
 
 
 def block_tables(extent):
@@ -82,12 +82,22 @@
 
 def pipeline_kernel(
     sections,
-    patches,
+    peers,
+    own_ref,
+    to_next_ref,
+    to_prior_ref,
     probe_ref,
     intensity_ref,
     tables_ref,
     kernel_ref,
     out_ref,
+    low_in,
+    high_in,
+    patches,
+    top_in,
+    bottom_in,
+    high_out,
+    low_out,
     psi_in,
     psi_out,
     chi_in,
@@ -99,17 +109,71 @@
     psi_recv,
     chi_send,
     chi_recv,
+    top_send,
+    top_recv,
+    bottom_send,
+    bottom_recv,
+    high_send,
+    high_recv,
+    low_send,
+    low_recv,
 ):
     section = lax.axis_index("depth")
+    scan = lax.axis_index("scan")
     final = sections - 1
+    has_prior, has_next = (scan > 0, scan < peers - 1)
     positions, extent = (out_ref.shape[0], out_ref.shape[-1])
+    half = extent // 2
     following = lax.rem(section + 1, sections)
     previous = lax.rem(section + sections - 1, sections)
 
     barrier = pltpu.get_barrier_semaphore()
     for neighbour in (previous, following):
         pl.semaphore_signal(barrier, inc=1, device_id={"depth": neighbour}, device_id_type=MESH)
-    pl.semaphore_wait(barrier, 2)
+    for exists, peer, empty in (
+        (has_prior, scan - 1, (top_in, low_in)),
+        (has_next, scan + 1, (bottom_in, high_in)),
+    ):
+
+        @pl.when(exists)
+        def _():
+            pl.semaphore_signal(barrier, inc=1, device_id={"scan": peer}, device_id_type=MESH)
+
+        @pl.when(jnp.logical_not(exists))
+        def _():
+            for ref in empty:
+                ref[...] = jnp.zeros_like(ref)
+
+    greeted = 2 + jnp.where(has_prior, 1, 0) + jnp.where(has_next, 1, 0)
+    pl.semaphore_wait(barrier, greeted)
+
+    def scan_copy(source, target, send, recv, step):
+        return lambda index: pltpu.make_async_remote_copy(
+            src_ref=source.at[index],
+            dst_ref=target.at[index],
+            send_sem=send.at[index],
+            recv_sem=recv.at[index],
+            device_id={"scan": scan + step},
+            device_id_type=MESH,
+        )
+
+    top_copy = scan_copy(to_next_ref, top_in, top_send, top_recv, 1)
+    bottom_copy = scan_copy(to_prior_ref, bottom_in, bottom_send, bottom_recv, -1)
+    high_copy = scan_copy(high_out, high_in, high_send, high_recv, -1)
+    low_copy = scan_copy(low_out, low_in, low_send, low_recv, 1)
+
+    def halo_send(index, carry):
+        @pl.when(has_next)
+        def _():
+            top_copy(index).start()
+
+        @pl.when(has_prior)
+        def _():
+            bottom_copy(index).start()
+
+        return carry
+
+    lax.fori_loop(0, positions, halo_send, 0)
 
     def psi_copy(index):
         return pltpu.make_async_remote_copy(
@@ -138,6 +202,18 @@
         return tables_ref[2], tables_ref[3]
 
     def forward_load(index):
+        @pl.when(has_prior)
+        def _():
+            top_copy(index).wait_recv()
+
+        @pl.when(has_next)
+        def _():
+            bottom_copy(index).wait_recv()
+
+        for part in range(2):
+            rims = jnp.concatenate([top_in[index, part], bottom_in[index, part]], axis=0)
+            patches[index, part] = own_ref[index, part] + rims.astype(jnp.float32)
+
         @pl.when(section == 0)
         def _():
             wave[index] = probe_ref[...]
@@ -184,6 +260,18 @@
         term = conj_times((wave[index, 0], wave[index, 1]), chi)
         for part in range(2):
             out_ref[index, part] = term[part]
+            rounded = term[part].astype(jnp.bfloat16)
+            high_out[index, part] = rounded[:half]
+            low_out[index, part] = rounded[half:]
+
+    def gradient_send(index):
+        @pl.when(has_prior)
+        def _():
+            high_copy(index).start()
+
+        @pl.when(has_next)
+        def _():
+            low_copy(index).start()
 
     def backward_compute(index):
         chi = (adjoint[0], adjoint[1])
@@ -218,6 +306,7 @@
         backward_compute(index)
         forward_send(step)
         backward_send(index)
+        gradient_send(index)
         return carry
 
     def backward_only(step, carry):
@@ -230,6 +319,7 @@
             backward_compute(index)
 
         backward_send(index)
+        gradient_send(index)
         return carry
 
     lax.fori_loop(0, lag, forward_only, 0)
@@ -245,22 +335,44 @@
         def _():
             chi_copy(index).wait_send()
 
+        @pl.when(has_prior)
+        def _():
+            bottom_copy(index).wait_send()
+            high_copy(index).wait_send()
+            low_copy(index).wait_recv()
+
+        @pl.when(has_next)
+        def _():
+            top_copy(index).wait_send()
+            low_copy(index).wait_send()
+            high_copy(index).wait_recv()
+
         return carry
 
     lax.fori_loop(0, positions, drain, 0)
 
 
-def pipeline(sections, patches, probe, intensity):
+def pipeline(sections, peers, own, to_next, to_prior, probe, intensity):
     positions, extent = (intensity.shape[0], intensity.shape[-1])
     vmem = pl.BlockSpec(memory_space=pltpu.VMEM)
     waves = (positions, 2, extent, extent)
+    halves = (positions, 2, extent // 2, extent)
     semaphores = pltpu.SemaphoreType.DMA((positions,))
     return pl.pallas_call(
-        functools.partial(pipeline_kernel, sections),
-        out_shape=jax.ShapeDtypeStruct(waves, jnp.float32),
-        in_specs=[vmem] * 5,
-        out_specs=vmem,
+        functools.partial(pipeline_kernel, sections, peers),
+        out_shape=[
+            jax.ShapeDtypeStruct(waves, jnp.float32),
+            jax.ShapeDtypeStruct(halves, jnp.bfloat16),
+            jax.ShapeDtypeStruct(halves, jnp.bfloat16),
+        ],
+        in_specs=[vmem] * 7,
+        out_specs=[vmem] * 3,
         scratch_shapes=[
+            pltpu.VMEM(waves, jnp.float32),
+            pltpu.VMEM(halves, HALO_TYPE),
+            pltpu.VMEM(halves, HALO_TYPE),
+            pltpu.VMEM(halves, jnp.bfloat16),
+            pltpu.VMEM(halves, jnp.bfloat16),
             pltpu.VMEM(waves, jnp.bfloat16),
             pltpu.VMEM(waves, jnp.bfloat16),
             pltpu.VMEM(waves, jnp.bfloat16),
@@ -268,16 +380,15 @@
             pltpu.VMEM(waves, jnp.float32),
             pltpu.VMEM((2, 2, extent, extent), jnp.float32),
             pltpu.VMEM((2, extent, extent), jnp.float32),
-            semaphores,
-            semaphores,
-            semaphores,
-            semaphores,
-        ],
+        ]
+        + [semaphores] * 12,
         compiler_params=pltpu.CompilerParams(
             collective_id=0, has_side_effects=True, vmem_limit_bytes=48 * 1024 * 1024
         ),
     )(
-        patches,
+        own,
+        to_next,
+        to_prior,
         probe,
         intensity,
         jnp.asarray(block_tables(extent)),
@@ -285,99 +396,117 @@
     )
 
 
-def cut_kernel(rows_ref, cols_ref, layer_ref, out_ref):
-    positions, extent = (out_ref.shape[0], out_ref.shape[-1])
-    columns = layer_ref.shape[-1]
+def cut_kernel(
+    rows_ref, cols_ref, next_rows, next_cols, prior_rows, prior_cols, layer_ref,
+    own_ref, to_next_ref, to_prior_ref, padded,
+):
+    positions, extent = (own_ref.shape[0], own_ref.shape[-1])
+    strip, columns = layer_ref.shape[1:]
+    zeros = jnp.zeros((2, strip, columns), jnp.float32)
+    padded[:, :strip] = zeros
+    padded[:, strip : 2 * strip] = layer_ref[...]
+    padded[:, 2 * strip :] = zeros
+
+    def take(out, index, row, column):
+        height = out.shape[2]
+        tall, wide = (height + 8, 2 * extent)
+        top, down = aligned_place(row, 8, padded.shape[1], tall)
+        start, shift = aligned_place(column, extent, columns, wide)
+        for part in range(2):
+            block = padded[part, pl.ds(top, tall), pl.ds(start, wide)]
+            block = pltpu.roll(block, lax.rem(wide - shift, wide), 1)[:, :extent]
+            block = pltpu.roll(block, lax.rem(tall - down, tall), 0)[:height]
+            out[index, part] = block.astype(out.dtype)
 
     def cut_window(index, carry):
-        tall, wide = (extent + 8, 2 * extent)
-        top, down = aligned_place(rows_ref[index], 8, layer_ref.shape[1], tall)
-        start, shift = aligned_place(cols_ref[index], extent, columns, wide)
-        for part in range(2):
-            block = layer_ref[part, pl.ds(top, tall), pl.ds(start, wide)]
-            block = pltpu.roll(block, lax.rem(wide - shift, wide), 1)[:, :extent]
-            out_ref[index, part] = pltpu.roll(block, lax.rem(tall - down, tall), 0)[:extent]
+        take(own_ref, index, rows_ref[index], cols_ref[index])
+        take(to_next_ref, index, strip + next_rows[index], next_cols[index])
+        take(to_prior_ref, index, prior_rows[index], prior_cols[index])
         return carry
 
     lax.fori_loop(0, positions, cut_window, 0)
 
 
-def cut(row_starts, col_starts, layer, extent):
+def cut(places, layer, extent):
     smem = pl.BlockSpec(memory_space=pltpu.SMEM)
     vmem = pl.BlockSpec(memory_space=pltpu.VMEM)
-    windows = (row_starts.shape[0], 2, extent, extent)
+    positions = places[0].shape[0]
+    strip, columns = layer.shape[1:]
+    halves = (positions, 2, extent // 2, extent)
     return pl.pallas_call(
         cut_kernel,
-        out_shape=jax.ShapeDtypeStruct(windows, jnp.float32),
-        in_specs=[smem, smem, vmem],
-        out_specs=vmem,
+        out_shape=[
+            jax.ShapeDtypeStruct((positions, 2, extent, extent), jnp.float32),
+            jax.ShapeDtypeStruct(halves, HALO_TYPE),
+            jax.ShapeDtypeStruct(halves, HALO_TYPE),
+        ],
+        in_specs=[smem] * 6 + [vmem],
+        out_specs=[vmem] * 3,
+        scratch_shapes=[pltpu.VMEM((2, 3 * strip, columns), jnp.float32)],
         compiler_params=pltpu.CompilerParams(vmem_limit_bytes=32 * 1024 * 1024),
-    )(row_starts, col_starts, layer)
-
-
-def scatter_kernel(rows_ref, cols_ref, terms_ref, middle_ref, upper_ref, lower_ref, grid):
+    )(*places, layer)
+
+
+def scatter_kernel(
+    rows_ref, cols_ref, next_rows, next_cols, prior_rows, prior_cols,
+    terms_ref, high_ref, low_ref, out_ref, grid,
+):
     positions, extent = (terms_ref.shape[0], terms_ref.shape[-1])
-    columns = grid.shape[-1]
-    strip = middle_ref.shape[1]
+    strip, columns = out_ref.shape[1:]
     grid[...] = jnp.zeros_like(grid)
 
-    def add_window(index, carry):
-        tall, wide = (extent + 8, 2 * extent)
-        top, down = aligned_place(rows_ref[index], 8, grid.shape[1], tall)
-        start, shift = aligned_place(cols_ref[index], extent, columns, wide)
+    def add(source, index, row, column):
+        height = source.shape[2]
+        tall, wide = (height + 8, 2 * extent)
+        top, down = aligned_place(row, 8, grid.shape[1], tall)
+        start, shift = aligned_place(column, extent, columns, wide)
         for part in range(2):
-            term = terms_ref[index, part]
+            term = source[index, part].astype(jnp.float32)
             term = jnp.concatenate([term, jnp.zeros((8, extent), term.dtype)], axis=0)
             term = pltpu.roll(term, down, 0)
             term = jnp.concatenate([term, jnp.zeros_like(term)], axis=1)
             place = (part, pl.ds(top, tall), pl.ds(start, wide))
             grid[place] = grid[place] + pltpu.roll(term, shift, 1)
-        return carry
-
-    lax.fori_loop(0, positions, add_window, 0)
-    upper_ref[...] = grid[:, :strip].astype(upper_ref.dtype)
-    middle_ref[...] = grid[:, strip : 2 * strip]
-    lower_ref[...] = grid[:, 2 * strip :].astype(lower_ref.dtype)
-
-
-def scatter(row_starts, col_starts, terms, strip, columns):
+
+    def add_windows(index, carry):
+        add(terms_ref, index, rows_ref[index], cols_ref[index])
+        add(high_ref, index, strip + next_rows[index], next_cols[index])
+        add(low_ref, index, prior_rows[index], prior_cols[index])
+        return carry
+
+    lax.fori_loop(0, positions, add_windows, 0)
+    out_ref[...] = grid[:, strip : 2 * strip]
+
+
+def scatter(places, terms, high, low, strip, columns):
     smem = pl.BlockSpec(memory_space=pltpu.SMEM)
     vmem = pl.BlockSpec(memory_space=pltpu.VMEM)
-    piece = (2, strip, columns)
     return pl.pallas_call(
         scatter_kernel,
-        out_shape=[
-            jax.ShapeDtypeStruct(piece, jnp.float32),
-            jax.ShapeDtypeStruct(piece, jnp.bfloat16),
-            jax.ShapeDtypeStruct(piece, jnp.bfloat16),
-        ],
-        in_specs=[smem, smem, vmem],
-        out_specs=[vmem, vmem, vmem],
+        out_shape=jax.ShapeDtypeStruct((2, strip, columns), jnp.float32),
+        in_specs=[smem] * 6 + [vmem] * 3,
+        out_specs=vmem,
         scratch_shapes=[pltpu.VMEM((2, 3 * strip, columns), jnp.float32)],
         compiler_params=pltpu.CompilerParams(vmem_limit_bytes=32 * 1024 * 1024),
-    )(row_starts, col_starts, terms)
-
-
-def shards(scan_peers, sections, object_slices, probe_wave, offsets, intensity):
+    )(*places, terms, high, low)
+
+
+def shards(peers, sections, object_slices, probe_wave, offsets, intensity):
     layer = object_slices[0]
     strip, columns = layer.shape[1:]
+    extent = probe_wave.shape[-1]
     scan_index = lax.axis_index("scan")
-    up = [(i, i + 1) for i in range(scan_peers - 1)]
+    up = [(i, i + 1) for i in range(peers - 1)]
     down = [(j, i) for i, j in up]
-    travelling = layer.astype(HALO_TYPE)
-    before = lax.ppermute(travelling, "scan", up)
-    after = lax.ppermute(travelling, "scan", down)
-    extended = jnp.concatenate(
-        [before.astype(jnp.float32), layer, after.astype(jnp.float32)], axis=1
+    starts = jnp.stack([offsets[:, 0] - (scan_index - 1) * strip, offsets[:, 1]])
+    after = lax.ppermute(starts, "scan", down)
+    before = lax.ppermute(starts, "scan", up)
+    places = [place[i] for place in (starts, after, before) for i in range(2)]
+    own, to_next, to_prior = cut(places, layer, extent)
+    terms, low, high = pipeline(
+        sections, peers, own, to_next, to_prior, probe_wave, intensity
     )
-    row_starts = offsets[:, 0] - (scan_index - 1) * strip
-    col_starts = offsets[:, 1]
-    patches = cut(row_starts, col_starts, extended, probe_wave.shape[-1])
-    terms = pipeline(sections, patches, probe_wave, intensity)
-    middle, upper, lower = scatter(row_starts, col_starts, terms, strip, columns)
-    from_below = lax.ppermute(lower, "scan", up).astype(jnp.float32)
-    from_above = lax.ppermute(upper, "scan", down).astype(jnp.float32)
-    return (middle + from_below + from_above)[None]
+    return scatter(places, terms, high, low, strip, columns)[None]
 
 
 def solution(mesh):

time: 120 us -> 104 us (0.87)
  waiting for transfers between devices: 41.7 us -> 4.14 us
  Pallas kernels: 61.5 us -> 86.2 us
  local copies, waits for them, and re-layouts: 0.03 us -> 6.63 us
  starting transfers between devices: 12.5 us -> 6.13 us
  other arithmetic: 3.65 us -> 0.77 us
    ppermute x4 -> x2, waiting for transfers between devices: 41.7 us -> 4.14 us  [the longest x1 4.14 us: shards(): after = lax.ppermute(starts, 'scan', down)]
    pallas_call x3, Pallas kernels: 61.5 us -> 86.2 us  [the longest x1 77.1 us: pipeline(): pl.pallas_call(functools.partial(pipeline_kernel, sections, peers), out_s...]
    unnamed x10 -> x12, local copies, waits for them, and re-layouts: 0.03 us -> 6.62 us
    ppermute x4 -> x2, starting transfers between devices: 12.5 us -> 6.13 us  [the longest x1 4.84 us: shards(): before = lax.ppermute(starts, 'scan', up)]
    convert_element_type x3 -> x0, other arithmetic: 1.51 us -> none  [the longest x1 1.37 us: shards(): travelling = layer.astype(HALO_TYPE)]
  transfers between devices with their start and end apart: 4 -> 2, of which waited for: 3 -> 1; matrix products, arithmetic and copies ran while one was open for 1% -> 0% of each run, Pallas kernels for 0% -> 0%
where the time goes in v1:
time: 104 us
  Pallas kernels  86.2 us (83%)
  local copies, waits for them, and re-layouts  6.63 us (6%)
  starting transfers between devices  6.13 us (6%)
  waiting for transfers between devices  4.14 us (4%)
    pallas_call x1, Pallas kernels, pipeline(): pl.pallas_call(functools.partial(pipeline_kernel, sections, peers), out_s...  77.1 us
    unnamed x12, local copies, waits for them, and re-layouts  6.62 us
    pallas_call x1, Pallas kernels, scatter(): pl.pallas_call(scatter_kernel, out_shape=jax.ShapeDtypeStruct((2, strip,...  4.87 us
    ppermute x1, starting transfers between devices, shards(): before = lax.ppermute(starts, 'scan', up)  4.84 us
    pallas_call x1, Pallas kernels, cut(): pl.pallas_call(cut_kernel, out_shape=[jax.ShapeDtypeStruct((positions, 2,...  4.3 us
    ppermute x1, waiting for transfers between devices, shards(): after = lax.ppermute(starts, 'scan', down)  4.14 us
  transfers between devices with their start and end apart: 2, of which 1 were waited for; matrix products, arithmetic and copies ran while one was open for 0% of the time, Pallas kernels for 0%

profile of v1, /device:TPU:0, one launch (start us, length us, event | category | flops | bytes accessed | tf_op | source)
XLA Modules:
  0.0 104.0 jit_solution(10947586987725218674)
XLA Ops:
  0.0 0.8 fusion
  0.8 4.8 %collective-permute-start.1 = (s32[2,16]{1,0:T(2,128)S(1)}, s32[2,16]{1,0:T(2,128)S(1)}, u32[]{:S(2)}, u32[]{:S(2)}) collective-permute-start(s32[2,16]{1,0:T(2,128)S(1)} %pad_add_fusion), channel_id=1, source_target_pairs={{0,4},{4,8},{8,12},{12,16},{16,20},{20,24},{24,28},{1,5},{5,9},{9,... | collective-permute-start | bytes 392 | tf_op jit(solution)/shard_map/ppermute | solution.py:503
  5.6 1.3 %collective-permute-start = (s32[2,16]{1,0:T(2,128)S(1)}, s32[2,16]{1,0:T(2,128)S(1)}, u32[]{:S(2)}, u32[]{:S(2)}) collective-permute-start(s32[2,16]{1,0:T(2,128)S(1)} %pad_add_fusion), channel_id=1, source_target_pairs={{4,0},{8,4},{12,8},{16,12},{20,16},{24,20},{28,24},{5,1},{9,5},{13... | collective-permute-start | bytes 392 | tf_op jit(solution)/shard_map/ppermute | solution.py:502
  6.9 0.0 collective-permute-done.1
  6.9 4.1 %collective-permute-done = s32[2,16]{1,0:T(2,128)S(1)} collective-permute-done((s32[2,16]{1,0:T(2,128)S(1)}, s32[2,16]{1,0:T(2,128)S(1)}, u32[]{:S(2)}, u32[]{:S(2)}) %collective-permute-start) | collective-permute-done | bytes 160 | tf_op jit(solution)/shard_map/ppermute | solution.py:502
  11.1 0.0 copy-start.2
  11.1 1.2 %copy-done.2 = f32[1,2,64,2048]{3,2,1,0:T(8,128)S(1)} copy-done((f32[1,2,64,2048]{3,2,1,0:T(8,128)S(1)}, f32[1,2,64,2048]{3,2,1,0:T(8,128)}, u32[]{:S(2)}) %copy-start.2) | copy-done | bytes 1048600
  12.3 4.3 %shard_map.64 = (f32[16,2,128,128]{3,2,1,0:T(8,128)S(1)}, bf16[16,2,64,128]{3,2,1,0:T(8,128)(2,1)S(1)}, bf16[16,2,64,128]{3,2,1,0:T(8,128)(2,1)S(1)}) custom-call(s32[16]{0:T(128)S(1)} %get-tuple-element.24.rows_ref, s32[16]{0:T(128)S(1)} %get-tuple-element.23.cols_ref, s32[16]{0:T(128)S(1)} %get-tuple-element.20.next_rows, ...), custom_call_target="tpu_custom_call" | custom-call | tf_op jit(solution)/shard_map/pallas_call | solution.py:436
  16.6 0.0 copy-start
  16.6 1.3 %copy-done = f32[16,2,128,128]{3,2,1,0:T(8,128)} copy-done((f32[16,2,128,128]{3,2,1,0:T(8,128)}, f32[16,2,128,128]{3,2,1,0:T(8,128)S(1)}, u32[]{:S(2)}) %copy-start) | copy-done | bytes 2097176
  18.0 0.0 copy-start.1
  18.0 1.2 %copy-done.1 = f32[16,128,128]{2,1,0:T(8,128)S(1)} copy-done((f32[16,128,128]{2,1,0:T(8,128)S(1)}, f32[16,128,128]{2,1,0:T(8,128)}, u32[]{:S(2)}) %copy-start.1) | copy-done | bytes 1048600
  19.2 0.0 copy-start.3
  19.2 1.0 copy-done.3
  20.2 0.0 copy-start.4
  20.2 0.9 copy-done.4
  21.1 0.0 copy-start.5
  21.1 0.9 copy-done.5
  22.0 77.1 %shard_map.65 = (f32[16,2,128,128]{3,2,1,0:T(8,128)S(1)}, bf16[16,2,64,128]{3,2,1,0:T(8,128)(2,1)S(1)}, bf16[16,2,64,128]{3,2,1,0:T(8,128)(2,1)S(1)}) custom-call(f32[16,2,128,128]{3,2,1,0:T(8,128)} %copy-done, bf16[16,2,64,128]{3,2,1,0:T(8,128)(2,1)S(1)} %get-tuple-element.12.to_next_ref, bf16[16,2,64,128]{3,2,1,0:T(8,128)(2,1)S(1)} %get-tuple-element.13.to_prior_ref, ...), custom_call_target="tpu_custom_call" | custom-call | tf_op jit(solution)/shard_map/pallas_call | solution.py:361
  99.1 4.9 %shard_map.66 = f32[2,64,2048]{2,1,0:T(8,128)} custom-call(s32[16]{0:T(128)S(1)} %get-tuple-element.24.rows_ref, s32[16]{0:T(128)S(1)} %get-tuple-element.23.cols_ref, s32[16]{0:T(128)S(1)} %get-tuple-element.20.next_rows, s32[16]{0:T(128)S(1)} %get-tuple-element.19.next_cols, s32[16]{0:T(128)S(1)} %get-tuple-element.18.prior_rows, ...), custom_call_target="tpu_custom_call" | custom-call | tf_op jit(solution)/shard_map/pallas_call | solution.py:484
  (3 shorter events, 0.0 us)
Async XLA Ops:
  0.8 6.2 %collective-permute-start.1 = (s32[2,16]{1,0:T(2,128)S(1)}, s32[2,16]{1,0:T(2,128)S(1)}, u32[]{:S(2)}, u32[]{:S(2)}) collective-permute-start(s32[2,16]{1,0:T(2,128)S(1)} %pad_add_fusion), channel_id=1, source_target_pairs={{0,4},{4,8},{8,12},{12,16},{16,20},{20,24},{24,28},{1,5},{5,9},{9,... | collective-permute-start | bytes 392 | tf_op jit(solution)/shard_map/ppermute | solution.py:503
  5.6 5.5 %collective-permute-start = (s32[2,16]{1,0:T(2,128)S(1)}, s32[2,16]{1,0:T(2,128)S(1)}, u32[]{:S(2)}, u32[]{:S(2)}) collective-permute-start(s32[2,16]{1,0:T(2,128)S(1)} %pad_add_fusion), channel_id=1, source_target_pairs={{4,0},{8,4},{12,8},{16,12},{20,16},{24,20},{28,24},{5,1},{9,5},{13... | collective-permute-start | bytes 392 | tf_op jit(solution)/shard_map/ppermute | solution.py:502
  11.1 1.2 %copy-start.2 = (f32[1,2,64,2048]{3,2,1,0:T(8,128)S(1)}, f32[1,2,64,2048]{3,2,1,0:T(8,128)}, u32[]{:S(2)}) copy-start(f32[1,2,64,2048]{3,2,1,0:T(8,128)} %param.6) | copy-start | bytes 3145732
  16.6 1.3 %copy-start = (f32[16,2,128,128]{3,2,1,0:T(8,128)}, f32[16,2,128,128]{3,2,1,0:T(8,128)S(1)}, u32[]{:S(2)}) copy-start(f32[16,2,128,128]{3,2,1,0:T(8,128)S(1)} %get-tuple-element.11.own_ref) | copy-start | bytes 6291460
  18.0 1.2 %copy-start.1 = (f32[16,128,128]{2,1,0:T(8,128)S(1)}, f32[16,128,128]{2,1,0:T(8,128)}, u32[]{:S(2)}) copy-start(f32[16,128,128]{2,1,0:T(8,128)} %intensity_ref.1) | copy-start | bytes 3145732
  19.2 1.0 %copy-start.3 = (bf16[4,256,256]{2,1,0:T(8,128)(2,1)S(1)}, bf16[4,256,256]{2,1,0:T(8,128)(2,1)}, u32[]{:S(2)}) copy-start(bf16[4,256,256]{2,1,0:T(8,128)(2,1)} %constant.15.clone.tables_ref) | copy-start | bytes 1572868
  20.2 0.9 copy-start.4
  21.1 0.9 copy-start.5

commit v2 on v1

--- a/solution.py
+++ b/solution.py
@@ -11,7 +11,7 @@
 
 FRESNEL = 0.0024
 MESH = pl.DeviceIdType.MESH
-HOP_LAG = 3
+HOP_LAG = 6
 HALO_TYPE = jnp.bfloat16
 
 
@@ -383,7 +383,7 @@
         ]
         + [semaphores] * 12,
         compiler_params=pltpu.CompilerParams(
-            collective_id=0, has_side_effects=True, vmem_limit_bytes=48 * 1024 * 1024
+            collective_id=0, has_side_effects=True, vmem_limit_bytes=24 * 1024 * 1024
         ),
     )(
         own,
@@ -443,7 +443,7 @@
         in_specs=[smem] * 6 + [vmem],
         out_specs=[vmem] * 3,
         scratch_shapes=[pltpu.VMEM((2, 3 * strip, columns), jnp.float32)],
-        compiler_params=pltpu.CompilerParams(vmem_limit_bytes=32 * 1024 * 1024),
+        compiler_params=pltpu.CompilerParams(vmem_limit_bytes=12 * 1024 * 1024),
     )(*places, layer)
 
 
@@ -487,7 +487,7 @@
         in_specs=[smem] * 6 + [vmem] * 3,
         out_specs=vmem,
         scratch_shapes=[pltpu.VMEM((2, 3 * strip, columns), jnp.float32)],
-        compiler_params=pltpu.CompilerParams(vmem_limit_bytes=32 * 1024 * 1024),
+        compiler_params=pltpu.CompilerParams(vmem_limit_bytes=12 * 1024 * 1024),
     )(*places, terms, high, low)
 
 

time: 104 us -> 88.9 us (0.85)
  Pallas kernels: 86.2 us -> 72.1 us
  local copies, waits for them, and re-layouts: 6.63 us -> 5.3 us
    pallas_call x1, Pallas kernels: 77.1 us -> 63 us  [pipeline(): pl.pallas_call(functools.partial(pipeline_kernel, sections, peers), out_s...]
    unnamed x12 -> x10, local copies, waits for them, and re-layouts: 6.62 us -> 5.29 us
where the time goes in v2:
time: 88.9 us; the launch traced here: 88.5 us
  Pallas kernels  72.1 us (81%)
  starting transfers between devices  6.13 us (7%)
  local copies, waits for them, and re-layouts  5.3 us (6%)
  waiting for transfers between devices  4.14 us (5%)
    pallas_call x1, Pallas kernels, pipeline(): pl.pallas_call(functools.partial(pipeline_kernel, sections, peers), out_s...  63 us
    unnamed x10, local copies, waits for them, and re-layouts  5.29 us
    pallas_call x1, Pallas kernels, scatter(): pl.pallas_call(scatter_kernel, out_shape=jax.ShapeDtypeStruct((2, strip,...  4.88 us
    ppermute x1, starting transfers between devices, shards(): before = lax.ppermute(starts, 'scan', up)  4.84 us
    pallas_call x1, Pallas kernels, cut(): pl.pallas_call(cut_kernel, out_shape=[jax.ShapeDtypeStruct((positions, 2,...  4.3 us
    ppermute x1, waiting for transfers between devices, shards(): after = lax.ppermute(starts, 'scan', down)  4.14 us
  transfers between devices with their start and end apart: 2, of which 1 were waited for; matrix products, arithmetic and copies ran while one was open for 0% of the time, Pallas kernels for 0%

profile of v2, /device:TPU:0, one launch (start us, length us, event | category | flops | bytes accessed | tf_op | source)
XLA Modules:
  0.0 88.5 jit_solution(8410269763267712617)
XLA Ops:
  0.0 0.8 fusion
  0.8 4.8 %collective-permute-start.1 = (s32[2,16]{1,0:T(2,128)S(1)}, s32[2,16]{1,0:T(2,128)S(1)}, u32[]{:S(2)}, u32[]{:S(2)}) collective-permute-start(s32[2,16]{1,0:T(2,128)S(1)} %pad_add_fusion), channel_id=1, source_target_pairs={{0,4},{4,8},{8,12},{12,16},{16,20},{20,24},{24,28},{1,5},{5,9},{9,... | collective-permute-start | bytes 392 | tf_op jit(solution)/shard_map/ppermute | solution.py:503
  5.6 1.3 %collective-permute-start = (s32[2,16]{1,0:T(2,128)S(1)}, s32[2,16]{1,0:T(2,128)S(1)}, u32[]{:S(2)}, u32[]{:S(2)}) collective-permute-start(s32[2,16]{1,0:T(2,128)S(1)} %pad_add_fusion), channel_id=1, source_target_pairs={{4,0},{8,4},{12,8},{16,12},{20,16},{24,20},{28,24},{5,1},{9,5},{13... | collective-permute-start | bytes 392 | tf_op jit(solution)/shard_map/ppermute | solution.py:502
  6.9 0.0 collective-permute-done.1
  6.9 4.1 %collective-permute-done = s32[2,16]{1,0:T(2,128)S(1)} collective-permute-done((s32[2,16]{1,0:T(2,128)S(1)}, s32[2,16]{1,0:T(2,128)S(1)}, u32[]{:S(2)}, u32[]{:S(2)}) %collective-permute-start) | collective-permute-done | bytes 160 | tf_op jit(solution)/shard_map/ppermute | solution.py:502
  11.1 0.0 copy-start.1
  11.1 1.2 %copy-done.1 = f32[1,2,64,2048]{3,2,1,0:T(8,128)S(1)} copy-done((f32[1,2,64,2048]{3,2,1,0:T(8,128)S(1)}, f32[1,2,64,2048]{3,2,1,0:T(8,128)}, u32[]{:S(2)}) %copy-start.1) | copy-done | bytes 1048600
  12.3 4.3 %shard_map.64 = (f32[16,2,128,128]{3,2,1,0:T(8,128)S(1)}, bf16[16,2,64,128]{3,2,1,0:T(8,128)(2,1)S(1)}, bf16[16,2,64,128]{3,2,1,0:T(8,128)(2,1)S(1)}) custom-call(s32[16]{0:T(128)S(1)} %get-tuple-element.24.rows_ref, s32[16]{0:T(128)S(1)} %get-tuple-element.23.cols_ref, s32[16]{0:T(128)S(1)} %get-tuple-element.20.next_rows, ...), custom_call_target="tpu_custom_call" | custom-call | tf_op jit(solution)/shard_map/pallas_call | solution.py:436
  16.6 0.0 copy-start
  16.6 1.2 %copy-done = f32[16,128,128]{2,1,0:T(8,128)S(1)} copy-done((f32[16,128,128]{2,1,0:T(8,128)S(1)}, f32[16,128,128]{2,1,0:T(8,128)}, u32[]{:S(2)}) %copy-start) | copy-done | bytes 1048600
  17.8 0.0 copy-start.2
  17.9 1.0 %copy-done.2 = bf16[4,256,256]{2,1,0:T(8,128)(2,1)S(1)} copy-done((bf16[4,256,256]{2,1,0:T(8,128)(2,1)S(1)}, bf16[4,256,256]{2,1,0:T(8,128)(2,1)}, u32[]{:S(2)}) %copy-start.2) | copy-done | bytes 524312
  18.9 0.0 copy-start.3
  18.9 0.9 %copy-done.3 = f32[2,128,128]{2,1,0:T(8,128)S(1)} copy-done((f32[2,128,128]{2,1,0:T(8,128)S(1)}, f32[2,128,128]{2,1,0:T(8,128)}, u32[]{:S(2)}) %copy-start.3) | copy-done | bytes 131096
  19.8 0.0 copy-start.4
  19.8 0.9 %copy-done.4 = f32[2,128,128]{2,1,0:T(8,128)S(1)} copy-done((f32[2,128,128]{2,1,0:T(8,128)S(1)}, f32[2,128,128]{2,1,0:T(8,128)}, u32[]{:S(2)}) %copy-start.4) | copy-done | bytes 131096
  20.7 63.0 %shard_map.65 = (f32[16,2,128,128]{3,2,1,0:T(8,128)S(1)}, bf16[16,2,64,128]{3,2,1,0:T(8,128)(2,1)S(1)}, bf16[16,2,64,128]{3,2,1,0:T(8,128)(2,1)S(1)}) custom-call(f32[16,2,128,128]{3,2,1,0:T(8,128)S(1)} %get-tuple-element.11.own_ref, bf16[16,2,64,128]{3,2,1,0:T(8,128)(2,1)S(1)} %get-tuple-element.12.to_next_ref, ...), custom_call_target="tpu_custom_call" | custom-call | tf_op jit(solution)/shard_map/pallas_call | solution.py:361
  83.7 4.9 %shard_map.66 = f32[2,64,2048]{2,1,0:T(8,128)} custom-call(s32[16]{0:T(128)S(1)} %get-tuple-element.24.rows_ref, s32[16]{0:T(128)S(1)} %get-tuple-element.23.cols_ref, s32[16]{0:T(128)S(1)} %get-tuple-element.20.next_rows, s32[16]{0:T(128)S(1)} %get-tuple-element.19.next_cols, s32[16]{0:T(128)S(1)} %get-tuple-element.18.prior_rows, ...), custom_call_target="tpu_custom_call" | custom-call | tf_op jit(solution)/shard_map/pallas_call | solution.py:484
  (3 shorter events, 0.0 us)
Async XLA Ops:
  0.8 6.2 %collective-permute-start.1 = (s32[2,16]{1,0:T(2,128)S(1)}, s32[2,16]{1,0:T(2,128)S(1)}, u32[]{:S(2)}, u32[]{:S(2)}) collective-permute-start(s32[2,16]{1,0:T(2,128)S(1)} %pad_add_fusion), channel_id=1, source_target_pairs={{0,4},{4,8},{8,12},{12,16},{16,20},{20,24},{24,28},{1,5},{5,9},{9,... | collective-permute-start | bytes 392 | tf_op jit(solution)/shard_map/ppermute | solution.py:503
  5.6 5.5 %collective-permute-start = (s32[2,16]{1,0:T(2,128)S(1)}, s32[2,16]{1,0:T(2,128)S(1)}, u32[]{:S(2)}, u32[]{:S(2)}) collective-permute-start(s32[2,16]{1,0:T(2,128)S(1)} %pad_add_fusion), channel_id=1, source_target_pairs={{4,0},{8,4},{12,8},{16,12},{20,16},{24,20},{28,24},{5,1},{9,5},{13... | collective-permute-start | bytes 392 | tf_op jit(solution)/shard_map/ppermute | solution.py:502
  11.1 1.2 %copy-start.1 = (f32[1,2,64,2048]{3,2,1,0:T(8,128)S(1)}, f32[1,2,64,2048]{3,2,1,0:T(8,128)}, u32[]{:S(2)}) copy-start(f32[1,2,64,2048]{3,2,1,0:T(8,128)} %param.6) | copy-start | bytes 3145732
  16.6 1.2 %copy-start = (f32[16,128,128]{2,1,0:T(8,128)S(1)}, f32[16,128,128]{2,1,0:T(8,128)}, u32[]{:S(2)}) copy-start(f32[16,128,128]{2,1,0:T(8,128)} %intensity_ref.1) | copy-start | bytes 3145732
  17.8 1.0 %copy-start.2 = (bf16[4,256,256]{2,1,0:T(8,128)(2,1)S(1)}, bf16[4,256,256]{2,1,0:T(8,128)(2,1)}, u32[]{:S(2)}) copy-start(bf16[4,256,256]{2,1,0:T(8,128)(2,1)} %constant.15.clone.tables_ref) | copy-start | bytes 1572868
  18.9 0.9 %copy-start.3 = (f32[2,128,128]{2,1,0:T(8,128)S(1)}, f32[2,128,128]{2,1,0:T(8,128)}, u32[]{:S(2)}) copy-start(f32[2,128,128]{2,1,0:T(8,128)} %probe_ref.1) | copy-start | bytes 393220
  19.8 0.9 %copy-start.4 = (f32[2,128,128]{2,1,0:T(8,128)S(1)}, f32[2,128,128]{2,1,0:T(8,128)}, u32[]{:S(2)}) copy-start(f32[2,128,128]{2,1,0:T(8,128)} %constant.16.clone.kernel_ref) | copy-start | bytes 393220

commit v3 on v2

--- a/solution.py
+++ b/solution.py
@@ -12,6 +12,8 @@
 FRESNEL = 0.0024
 MESH = pl.DeviceIdType.MESH
 HOP_LAG = 6
+AHEAD = 4
+BEHIND = 3
 HALO_TYPE = jnp.bfloat16
 
 
@@ -84,20 +86,22 @@
     sections,
     peers,
     own_ref,
-    to_next_ref,
-    to_prior_ref,
+    mine_ref,
+    relay_ref,
+    pack_ref,
+    unpack_ref,
     probe_ref,
     intensity_ref,
     tables_ref,
     kernel_ref,
     out_ref,
-    low_in,
-    high_in,
+    near_in,
+    far_in,
     patches,
-    top_in,
-    bottom_in,
-    high_out,
-    low_out,
+    relay_in,
+    joined,
+    joined_in,
+    packed_out,
     psi_in,
     psi_out,
     chi_in,
@@ -109,30 +113,35 @@
     psi_recv,
     chi_send,
     chi_recv,
-    top_send,
-    top_recv,
-    bottom_send,
-    bottom_recv,
-    high_send,
-    high_recv,
-    low_send,
-    low_recv,
+    relay_send,
+    relay_recv,
+    join_send,
+    join_recv,
+    pack_send,
+    pack_recv,
+    onward_send,
+    onward_recv,
 ):
     section = lax.axis_index("depth")
     scan = lax.axis_index("scan")
     final = sections - 1
-    has_prior, has_next = (scan > 0, scan < peers - 1)
+    even = lax.rem(scan, 2) == 0
+    partner = jnp.where(even, scan + 1, scan - 1)
+    outward = jnp.where(even, scan - 2, scan + 2)
+    inward = jnp.where(even, scan + 2, scan - 2)
+    has_outward = (outward >= 0) & (outward < peers)
+    has_inward = (inward >= 0) & (inward < peers)
     positions, extent = (out_ref.shape[0], out_ref.shape[-1])
-    half = extent // 2
     following = lax.rem(section + 1, sections)
     previous = lax.rem(section + sections - 1, sections)
 
     barrier = pltpu.get_barrier_semaphore()
     for neighbour in (previous, following):
         pl.semaphore_signal(barrier, inc=1, device_id={"depth": neighbour}, device_id_type=MESH)
+    pl.semaphore_signal(barrier, inc=1, device_id={"scan": partner}, device_id_type=MESH)
     for exists, peer, empty in (
-        (has_prior, scan - 1, (top_in, low_in)),
-        (has_next, scan + 1, (bottom_in, high_in)),
+        (has_outward, outward, far_in),
+        (has_inward, inward, relay_in),
     ):
 
         @pl.when(exists)
@@ -141,39 +150,55 @@
 
         @pl.when(jnp.logical_not(exists))
         def _():
-            for ref in empty:
-                ref[...] = jnp.zeros_like(ref)
-
-    greeted = 2 + jnp.where(has_prior, 1, 0) + jnp.where(has_next, 1, 0)
+            empty[...] = jnp.zeros_like(empty)
+
+    greeted = 3 + jnp.where(has_outward, 1, 0) + jnp.where(has_inward, 1, 0)
     pl.semaphore_wait(barrier, greeted)
 
-    def scan_copy(source, target, send, recv, step):
+    def scan_copy(source, target, send, recv, peer):
         return lambda index: pltpu.make_async_remote_copy(
             src_ref=source.at[index],
             dst_ref=target.at[index],
             send_sem=send.at[index],
             recv_sem=recv.at[index],
-            device_id={"scan": scan + step},
+            device_id={"scan": peer},
             device_id_type=MESH,
         )
 
-    top_copy = scan_copy(to_next_ref, top_in, top_send, top_recv, 1)
-    bottom_copy = scan_copy(to_prior_ref, bottom_in, bottom_send, bottom_recv, -1)
-    high_copy = scan_copy(high_out, high_in, high_send, high_recv, -1)
-    low_copy = scan_copy(low_out, low_in, low_send, low_recv, 1)
-
-    def halo_send(index, carry):
-        @pl.when(has_next)
-        def _():
-            top_copy(index).start()
-
-        @pl.when(has_prior)
-        def _():
-            bottom_copy(index).start()
-
-        return carry
-
-    lax.fori_loop(0, positions, halo_send, 0)
+    relay_copy = scan_copy(relay_ref, relay_in, relay_send, relay_recv, outward)
+    join_copy = scan_copy(joined, joined_in, join_send, join_recv, partner)
+    pack_copy = scan_copy(packed_out, near_in, pack_send, pack_recv, partner)
+    onward_copy = scan_copy(near_in, far_in, onward_send, onward_recv, inward)
+
+    def relay_start(index, carry):
+        @pl.when(has_outward)
+        def _():
+            relay_copy(index).start()
+
+        return carry
+
+    def join(index, carry):
+        @pl.when(has_inward)
+        def _():
+            relay_copy(index).wait_recv()
+
+        joined[index] = relay_in[index] + mine_ref[index]
+        join_copy(index).start()
+        return carry
+
+    def onward(index, carry):
+        pack_copy(index).wait_recv()
+
+        @pl.when(has_inward)
+        def _():
+            onward_copy(index).start()
+
+        return carry
+
+    ahead = min(AHEAD, positions)
+    behind = min(BEHIND, positions)
+    lax.fori_loop(0, positions, relay_start, 0)
+    lax.fori_loop(0, ahead, join, 0)
 
     def psi_copy(index):
         return pltpu.make_async_remote_copy(
@@ -202,17 +227,14 @@
         return tables_ref[2], tables_ref[3]
 
     def forward_load(index):
-        @pl.when(has_prior)
-        def _():
-            top_copy(index).wait_recv()
-
-        @pl.when(has_next)
-        def _():
-            bottom_copy(index).wait_recv()
-
-        for part in range(2):
-            rims = jnp.concatenate([top_in[index, part], bottom_in[index, part]], axis=0)
-            patches[index, part] = own_ref[index, part] + rims.astype(jnp.float32)
+        @pl.when(index + ahead < positions)
+        def _():
+            join(index + ahead, 0)
+
+        join_copy(index).wait_recv()
+        for part in range(2):
+            rims = dot(unpack_ref[index], joined_in[index, part])
+            patches[index, part] = own_ref[index, part] + rims
 
         @pl.when(section == 0)
         def _():
@@ -260,18 +282,15 @@
         term = conj_times((wave[index, 0], wave[index, 1]), chi)
         for part in range(2):
             out_ref[index, part] = term[part]
-            rounded = term[part].astype(jnp.bfloat16)
-            high_out[index, part] = rounded[:half]
-            low_out[index, part] = rounded[half:]
+            rims = dot(pack_ref[index], term[part].astype(jnp.bfloat16))
+            packed_out[index, part] = rims.astype(jnp.bfloat16)
 
     def gradient_send(index):
-        @pl.when(has_prior)
-        def _():
-            high_copy(index).start()
-
-        @pl.when(has_next)
-        def _():
-            low_copy(index).start()
+        pack_copy(index).start()
+
+        @pl.when(index >= behind)
+        def _():
+            onward(index - behind, 0)
 
     def backward_compute(index):
         chi = (adjoint[0], adjoint[1])
@@ -326,7 +345,12 @@
     lax.fori_loop(lag, positions, both, 0)
     lax.fori_loop(positions, positions + lag, backward_only, 0)
 
+    lax.fori_loop(positions - behind, positions, onward, 0)
+
     def drain(index, carry):
+        join_copy(index).wait_send()
+        pack_copy(index).wait_send()
+
         @pl.when(section < final)
         def _():
             psi_copy(index).wait_send()
@@ -335,24 +359,21 @@
         def _():
             chi_copy(index).wait_send()
 
-        @pl.when(has_prior)
-        def _():
-            bottom_copy(index).wait_send()
-            high_copy(index).wait_send()
-            low_copy(index).wait_recv()
-
-        @pl.when(has_next)
-        def _():
-            top_copy(index).wait_send()
-            low_copy(index).wait_send()
-            high_copy(index).wait_recv()
+        @pl.when(has_outward)
+        def _():
+            relay_copy(index).wait_send()
+            onward_copy(index).wait_recv()
+
+        @pl.when(has_inward)
+        def _():
+            onward_copy(index).wait_send()
 
         return carry
 
     lax.fori_loop(0, positions, drain, 0)
 
 
-def pipeline(sections, peers, own, to_next, to_prior, probe, intensity):
+def pipeline(sections, peers, pieces, probe, intensity):
     positions, extent = (intensity.shape[0], intensity.shape[-1])
     vmem = pl.BlockSpec(memory_space=pltpu.VMEM)
     waves = (positions, 2, extent, extent)
@@ -365,7 +386,7 @@
             jax.ShapeDtypeStruct(halves, jnp.bfloat16),
             jax.ShapeDtypeStruct(halves, jnp.bfloat16),
         ],
-        in_specs=[vmem] * 7,
+        in_specs=[vmem] * 9,
         out_specs=[vmem] * 3,
         scratch_shapes=[
             pltpu.VMEM(waves, jnp.float32),
@@ -386,9 +407,7 @@
             collective_id=0, has_side_effects=True, vmem_limit_bytes=24 * 1024 * 1024
         ),
     )(
-        own,
-        to_next,
-        to_prior,
+        *pieces,
         probe,
         intensity,
         jnp.asarray(block_tables(extent)),
@@ -396,32 +415,50 @@
     )
 
 
+def kept_rows(shape, row, above):
+    inside = lax.broadcasted_iota(jnp.int32, shape, 0) >= row
+    return inside.astype(jnp.int32) == above
+
+
 def cut_kernel(
-    rows_ref, cols_ref, next_rows, next_cols, prior_rows, prior_cols, layer_ref,
-    own_ref, to_next_ref, to_prior_ref, padded,
+    rows_ref, cols_ref, near_rows, near_cols, far_rows, far_cols, even_ref, layer_ref,
+    own_ref, mine_ref, relay_ref, pack_ref, unpack_ref, padded,
 ):
     positions, extent = (own_ref.shape[0], own_ref.shape[-1])
     strip, columns = layer_ref.shape[1:]
+    wide = 2 * extent
     zeros = jnp.zeros((2, strip, columns), jnp.float32)
     padded[:, :strip] = zeros
     padded[:, strip : 2 * strip] = layer_ref[...]
     padded[:, 2 * strip :] = zeros
 
-    def take(out, index, row, column):
-        height = out.shape[2]
-        tall, wide = (height + 8, 2 * extent)
+    def take(out, index, row, column, above):
+        start, shift = aligned_place(column, extent, columns, wide)
+        keep = kept_rows((strip, extent), row, above)
+        for part in range(2):
+            block = layer_ref[part, :, pl.ds(start, wide)]
+            block = pltpu.roll(block, lax.rem(wide - shift, wide), 1)[:, :extent]
+            out[index, part] = jnp.where(keep, block, 0.0).astype(out.dtype)
+
+    def cut_window(index, carry):
+        tall = extent + 8
+        row = rows_ref[index]
         top, down = aligned_place(row, 8, padded.shape[1], tall)
-        start, shift = aligned_place(column, extent, columns, wide)
+        start, shift = aligned_place(cols_ref[index], extent, columns, wide)
         for part in range(2):
             block = padded[part, pl.ds(top, tall), pl.ds(start, wide)]
             block = pltpu.roll(block, lax.rem(wide - shift, wide), 1)[:, :extent]
-            block = pltpu.roll(block, lax.rem(tall - down, tall), 0)[:height]
-            out[index, part] = block.astype(out.dtype)
-
-    def cut_window(index, carry):
-        take(own_ref, index, rows_ref[index], cols_ref[index])
-        take(to_next_ref, index, strip + next_rows[index], next_cols[index])
-        take(to_prior_ref, index, prior_rows[index], prior_cols[index])
+            own_ref[index, part] = pltpu.roll(block, lax.rem(tall - down, tall), 0)[:extent]
+        even = even_ref[0]
+        take(mine_ref, index, near_rows[index], near_cols[index], even)
+        take(relay_ref, index, far_rows[index], far_cols[index], 1 - even)
+        for ref, strip_axis in ((pack_ref, 0), (unpack_ref, 1)):
+            shape = ref.shape[1:]
+            strip_row = lax.broadcasted_iota(jnp.int32, shape, strip_axis)
+            window_row = lax.broadcasted_iota(jnp.int32, shape, 1 - strip_axis)
+            distance = window_row - strip_row + row
+            hit = (distance == 0) | (distance == extent)
+            ref[index] = jnp.where(hit, 1.0, 0.0).astype(ref.dtype)
         return carry
 
     lax.fori_loop(0, positions, cut_window, 0)
@@ -439,17 +476,19 @@
             jax.ShapeDtypeStruct((positions, 2, extent, extent), jnp.float32),
             jax.ShapeDtypeStruct(halves, HALO_TYPE),
             jax.ShapeDtypeStruct(halves, HALO_TYPE),
+            jax.ShapeDtypeStruct((positions, extent // 2, extent), jnp.bfloat16),
+            jax.ShapeDtypeStruct((positions, extent, extent // 2), jnp.bfloat16),
         ],
-        in_specs=[smem] * 6 + [vmem],
-        out_specs=[vmem] * 3,
+        in_specs=[smem] * 7 + [vmem],
+        out_specs=[vmem] * 5,
         scratch_shapes=[pltpu.VMEM((2, 3 * strip, columns), jnp.float32)],
         compiler_params=pltpu.CompilerParams(vmem_limit_bytes=12 * 1024 * 1024),
     )(*places, layer)
 
 
 def scatter_kernel(
-    rows_ref, cols_ref, next_rows, next_cols, prior_rows, prior_cols,
-    terms_ref, high_ref, low_ref, out_ref, grid,
+    rows_ref, cols_ref, near_rows, near_cols, far_rows, far_cols, even_ref,
+    terms_ref, near_ref, far_ref, out_ref, grid,
 ):
     positions, extent = (terms_ref.shape[0], terms_ref.shape[-1])
     strip, columns = out_ref.shape[1:]
@@ -468,27 +507,38 @@
             place = (part, pl.ds(top, tall), pl.ds(start, wide))
             grid[place] = grid[place] + pltpu.roll(term, shift, 1)
 
+    def add_rows(source, index, row, column, above):
+        wide = 2 * extent
+        start, shift = aligned_place(column, extent, columns, wide)
+        keep = kept_rows((strip, extent), row, above)
+        for part in range(2):
+            term = jnp.where(keep, source[index, part].astype(jnp.float32), 0.0)
+            term = jnp.concatenate([term, jnp.zeros_like(term)], axis=1)
+            place = (part, pl.ds(strip, strip), pl.ds(start, wide))
+            grid[place] = grid[place] + pltpu.roll(term, shift, 1)
+
     def add_windows(index, carry):
+        even = even_ref[0]
         add(terms_ref, index, rows_ref[index], cols_ref[index])
-        add(high_ref, index, strip + next_rows[index], next_cols[index])
-        add(low_ref, index, prior_rows[index], prior_cols[index])
+        add_rows(near_ref, index, near_rows[index], near_cols[index], even)
+        add_rows(far_ref, index, far_rows[index], far_cols[index], 1 - even)
         return carry
 
     lax.fori_loop(0, positions, add_windows, 0)
     out_ref[...] = grid[:, strip : 2 * strip]
 
 
-def scatter(places, terms, high, low, strip, columns):
+def scatter(places, terms, near, far, strip, columns):
     smem = pl.BlockSpec(memory_space=pltpu.SMEM)
     vmem = pl.BlockSpec(memory_space=pltpu.VMEM)
     return pl.pallas_call(
         scatter_kernel,
         out_shape=jax.ShapeDtypeStruct((2, strip, columns), jnp.float32),
-        in_specs=[smem] * 6 + [vmem] * 3,
+        in_specs=[smem] * 7 + [vmem] * 3,
         out_specs=vmem,
         scratch_shapes=[pltpu.VMEM((2, 3 * strip, columns), jnp.float32)],
         compiler_params=pltpu.CompilerParams(vmem_limit_bytes=12 * 1024 * 1024),
-    )(*places, terms, high, low)
+    )(*places, terms, near, far)
 
 
 def shards(peers, sections, object_slices, probe_wave, offsets, intensity):
@@ -501,12 +551,14 @@
     starts = jnp.stack([offsets[:, 0] - (scan_index - 1) * strip, offsets[:, 1]])
     after = lax.ppermute(starts, "scan", down)
     before = lax.ppermute(starts, "scan", up)
-    places = [place[i] for place in (starts, after, before) for i in range(2)]
-    own, to_next, to_prior = cut(places, layer, extent)
-    terms, low, high = pipeline(
-        sections, peers, own, to_next, to_prior, probe_wave, intensity
-    )
-    return scatter(places, terms, high, low, strip, columns)[None]
+    even = lax.rem(scan_index, 2) == 0
+    near = jnp.where(even, after, before)
+    far = jnp.where(even, before, after)
+    places = [place[i] for place in (starts, near, far) for i in range(2)]
+    places.append(jnp.where(even, 1, 0).reshape(1))
+    pieces = cut(places, layer, extent)
+    terms, near_terms, far_terms = pipeline(sections, peers, pieces, probe_wave, intensity)
+    return scatter(places, terms, near_terms, far_terms, strip, columns)[None]
 
 
 def solution(mesh):

time: 88.9 us -> 87.7 us (0.987)
  Pallas kernels: 72.1 us -> 70.9 us
    pallas_call x1, Pallas kernels: 63 us -> 62 us  [pipeline(): pl.pallas_call(functools.partial(pipeline_kernel, sections, peers), out_s...]
where the time goes in v3:
time: 87.7 us; the launch traced here: 87.4 us
  Pallas kernels  70.9 us (81%)
  starting transfers between devices  6.13 us (7%)
  local copies, waits for them, and re-layouts  5.29 us (6%)
  waiting for transfers between devices  4.15 us (5%)
    pallas_call x1, Pallas kernels, pipeline(): pl.pallas_call(functools.partial(pipeline_kernel, sections, peers), out_s...  62 us
    unnamed x10, local copies, waits for them, and re-layouts  5.29 us
    ppermute x1, starting transfers between devices, shards(): before = lax.ppermute(starts, 'scan', up)  4.84 us
    pallas_call x1, Pallas kernels, scatter(): pl.pallas_call(scatter_kernel, out_shape=jax.ShapeDtypeStruct((2, strip,...  4.56 us
    pallas_call x1, Pallas kernels, cut(): pl.pallas_call(cut_kernel, out_shape=[jax.ShapeDtypeStruct((positions, 2,...  4.42 us
    ppermute x1, waiting for transfers between devices, shards(): after = lax.ppermute(starts, 'scan', down)  4.14 us
  transfers between devices with their start and end apart: 2, of which 1 were waited for; matrix products, arithmetic and copies ran while one was open for 0% of the time, Pallas kernels for 0%

profile of v3, /device:TPU:0, one launch (start us, length us, event | category | flops | bytes accessed | tf_op | source)
XLA Modules:
  0.0 87.4 jit_solution(10116432221766033545)
XLA Ops:
  0.0 0.8 fusion
  0.8 4.8 %collective-permute-start.1 = (s32[2,16]{1,0:T(2,128)S(1)}, s32[2,16]{1,0:T(2,128)S(1)}, u32[]{:S(2)}, u32[]{:S(2)}) collective-permute-start(s32[2,16]{1,0:T(2,128)S(1)} %pad_add_fusion), channel_id=1, source_target_pairs={{0,4},{4,8},{8,12},{12,16},{16,20},{20,24},{24,28},{1,5},{5,9},{9,... | collective-permute-start | bytes 392 | tf_op jit(solution)/shard_map/ppermute | solution.py:553
  5.6 1.3 %collective-permute-start = (s32[2,16]{1,0:T(2,128)S(1)}, s32[2,16]{1,0:T(2,128)S(1)}, u32[]{:S(2)}, u32[]{:S(2)}) collective-permute-start(s32[2,16]{1,0:T(2,128)S(1)} %pad_add_fusion), channel_id=1, source_target_pairs={{4,0},{8,4},{12,8},{16,12},{20,16},{24,20},{28,24},{5,1},{9,5},{13... | collective-permute-start | bytes 392 | tf_op jit(solution)/shard_map/ppermute | solution.py:552
  6.9 0.0 collective-permute-done.1
  6.9 4.1 %collective-permute-done = s32[2,16]{1,0:T(2,128)S(1)} collective-permute-done((s32[2,16]{1,0:T(2,128)S(1)}, s32[2,16]{1,0:T(2,128)S(1)}, u32[]{:S(2)}, u32[]{:S(2)}) %collective-permute-start) | collective-permute-done | bytes 160 | tf_op jit(solution)/shard_map/ppermute | solution.py:552
  11.1 0.0 copy-start
  11.1 1.2 %copy-done = f32[1,2,64,2048]{3,2,1,0:T(8,128)S(1)} copy-done((f32[1,2,64,2048]{3,2,1,0:T(8,128)S(1)}, f32[1,2,64,2048]{3,2,1,0:T(8,128)}, u32[]{:S(2)}) %copy-start) | copy-done | bytes 1048600
  12.3 4.4 %shard_map.64 = (f32[16,2,128,128]{3,2,1,0:T(8,128)S(1)}, bf16[16,2,64,128]{3,2,1,0:T(8,128)(2,1)S(1)}, bf16[16,2,64,128]{3,2,1,0:T(8,128)(2,1)S(1)}, bf16[16,64...) custom-call(s32[16]{0:T(128)S(1)} %get-tuple-element.30.rows_ref, s32[16]{0:T(128)S(1)} %get-tuple-element.29.cols_ref, ...), custom_call_target="tpu_custom_call" | custom-call | tf_op jit(solution)/shard_map/pallas_call | solution.py:473
  16.7 0.0 copy-start.1
  16.8 1.2 %copy-done.1 = f32[16,128,128]{2,1,0:T(8,128)S(1)} copy-done((f32[16,128,128]{2,1,0:T(8,128)S(1)}, f32[16,128,128]{2,1,0:T(8,128)}, u32[]{:S(2)}) %copy-start.1) | copy-done | bytes 1048600
  18.0 0.0 copy-start.2
  18.0 1.0 %copy-done.2 = bf16[4,256,256]{2,1,0:T(8,128)(2,1)S(1)} copy-done((bf16[4,256,256]{2,1,0:T(8,128)(2,1)S(1)}, bf16[4,256,256]{2,1,0:T(8,128)(2,1)}, u32[]{:S(2)}) %copy-start.2) | copy-done | bytes 524312
  19.0 0.0 copy-start.3
  19.0 0.9 %copy-done.3 = f32[2,128,128]{2,1,0:T(8,128)S(1)} copy-done((f32[2,128,128]{2,1,0:T(8,128)S(1)}, f32[2,128,128]{2,1,0:T(8,128)}, u32[]{:S(2)}) %copy-start.3) | copy-done | bytes 131096
  19.9 0.0 copy-start.4
  19.9 0.9 %copy-done.4 = f32[2,128,128]{2,1,0:T(8,128)S(1)} copy-done((f32[2,128,128]{2,1,0:T(8,128)S(1)}, f32[2,128,128]{2,1,0:T(8,128)}, u32[]{:S(2)}) %copy-start.4) | copy-done | bytes 131096
  20.8 62.0 %shard_map.65 = (f32[16,2,128,128]{3,2,1,0:T(8,128)S(1)}, bf16[16,2,64,128]{3,2,1,0:T(8,128)(2,1)S(1)}, bf16[16,2,64,128]{3,2,1,0:T(8,128)(2,1)S(1)}) custom-call(f32[16,2,128,128]{3,2,1,0:T(8,128)S(1)} %get-tuple-element.13.own_ref, bf16[16,2,64,128]{3,2,1,0:T(8,128)(2,1)S(1)} %get-tuple-element.14.mine_ref, ...), custom_call_target="tpu_custom_call" | custom-call | tf_op jit(solution)/shard_map/pallas_call | solution.py:382
  82.8 4.6 %shard_map.66 = f32[2,64,2048]{2,1,0:T(8,128)} custom-call(s32[16]{0:T(128)S(1)} %get-tuple-element.30.rows_ref, s32[16]{0:T(128)S(1)} %get-tuple-element.29.cols_ref, s32[16]{0:T(128)S(1)} %get-tuple-element.31.near_rows, s32[16]{0:T(128)S(1)} %get-tuple-element.32.near_cols, s32[16]{0:T(128)S(1)} %get-tuple-element.24.far_rows, ...), custom_call_target="tpu_custom_call" | custom-call | tf_op jit(solution)/shard_map/pallas_call | solution.py:534
  (3 shorter events, 0.0 us)
Async XLA Ops:
  0.8 6.2 %collective-permute-start.1 = (s32[2,16]{1,0:T(2,128)S(1)}, s32[2,16]{1,0:T(2,128)S(1)}, u32[]{:S(2)}, u32[]{:S(2)}) collective-permute-start(s32[2,16]{1,0:T(2,128)S(1)} %pad_add_fusion), channel_id=1, source_target_pairs={{0,4},{4,8},{8,12},{12,16},{16,20},{20,24},{24,28},{1,5},{5,9},{9,... | collective-permute-start | bytes 392 | tf_op jit(solution)/shard_map/ppermute | solution.py:553
  5.6 5.5 %collective-permute-start = (s32[2,16]{1,0:T(2,128)S(1)}, s32[2,16]{1,0:T(2,128)S(1)}, u32[]{:S(2)}, u32[]{:S(2)}) collective-permute-start(s32[2,16]{1,0:T(2,128)S(1)} %pad_add_fusion), channel_id=1, source_target_pairs={{4,0},{8,4},{12,8},{16,12},{20,16},{24,20},{28,24},{5,1},{9,5},{13... | collective-permute-start | bytes 392 | tf_op jit(solution)/shard_map/ppermute | solution.py:552
  11.1 1.2 %copy-start = (f32[1,2,64,2048]{3,2,1,0:T(8,128)S(1)}, f32[1,2,64,2048]{3,2,1,0:T(8,128)}, u32[]{:S(2)}) copy-start(f32[1,2,64,2048]{3,2,1,0:T(8,128)} %param.6) | copy-start | bytes 3145732
  16.7 1.2 %copy-start.1 = (f32[16,128,128]{2,1,0:T(8,128)S(1)}, f32[16,128,128]{2,1,0:T(8,128)}, u32[]{:S(2)}) copy-start(f32[16,128,128]{2,1,0:T(8,128)} %intensity_ref.1) | copy-start | bytes 3145732
  18.0 1.0 %copy-start.2 = (bf16[4,256,256]{2,1,0:T(8,128)(2,1)S(1)}, bf16[4,256,256]{2,1,0:T(8,128)(2,1)}, u32[]{:S(2)}) copy-start(bf16[4,256,256]{2,1,0:T(8,128)(2,1)} %constant.21.clone.tables_ref) | copy-start | bytes 1572868
  19.0 0.9 %copy-start.3 = (f32[2,128,128]{2,1,0:T(8,128)S(1)}, f32[2,128,128]{2,1,0:T(8,128)}, u32[]{:S(2)}) copy-start(f32[2,128,128]{2,1,0:T(8,128)} %probe_ref.1) | copy-start | bytes 393220
  19.9 0.9 %copy-start.4 = (f32[2,128,128]{2,1,0:T(8,128)S(1)}, f32[2,128,128]{2,1,0:T(8,128)}, u32[]{:S(2)}) copy-start(f32[2,128,128]{2,1,0:T(8,128)} %constant.22.clone.kernel_ref) | copy-start | bytes 393220
